TPU v7x, 32 devices: a whole 2x2x4 slice. The times are simulated.
32 devices in a mesh: roll: 4 (over y, x), seq: 8 (over z, core).
Axes of the slice: x: 2, y: 2, z: 4, core: 2. Of those that a mesh axis runs over, the one named last changes fastest.
Arguments:
- query_rows: bfloat16 [4, 4096, 1792], P('roll', 'seq'), may hold values from -200 to 200
- key_rows: bfloat16 [4, 4096, 256], P('roll', 'seq'), may hold values from -6 to 6
- value_rows: bfloat16 [4, 4096, 256], P('roll', 'seq'), may hold values from -6 to 6
- cotangent: bfloat16 [4, 4096, 1792], P('roll', None, 'seq'), may hold values from -6 to 6
- slopes: float32 [14], replicated, may hold values from 0.00029296876 to 0.0390625
- lengths: int32 [4], P('roll'), may hold values from 1024 to 4096, as said below
- loss_mask: int32 [4, 4096], P('roll', 'seq'), may hold values 0 or 1
- distances: int32 [4], P('roll'), may hold values from 40 to 357
Outputs:
- grad_queries: bfloat16 [4, 4096, 1792], P('roll', 'seq')
- grad_keys: bfloat16 [4, 4096, 256], P('roll', 'seq')
- grad_values: bfloat16 [4, 4096, 256], P('roll', 'seq')
Inputs may be any that keep to these rules, and one draw needn't show every extreme that they name: `lengths`: some rollout has 4096 tokens and some 4096 // 4.
All inputs are finite; a program needn't handle non-finite values. No bound on the sum of `loss_mask` on one device may be relied on, other than what follows from the above.
Results may differ from a plain program's by a relative error of at most 0.0068.
Values may be sent and summed in bfloat16 or wider, within the bound.
No kernel may reach another device: no remote copies, remote signals or barrier semaphores. Data moves between devices by JAX's collectives and lax.ppermute only.
A program may use at most 64 MiB of HBM per device.

v0:
```python
import math
import jax
import jax.numpy as jnp
from jax import lax
from jax.sharding import PartitionSpec as P

HEAD_DIM = 128
WINDOW = 1024


def passed_along(value, axis, steps):
    count = lax.axis_size(axis)
    leading, last = (max(0, -steps), min(count, count - steps))
    return lax.ppermute(value, axis, [(source, source + steps) for source in range(leading, last)])


def shards(query_rows, key_rows, value_rows, cotangent, slopes, lengths, loss_mask, distances):
    own_q = query_rows[0]
    own_k = key_rows[0]
    own_v = value_rows[0]
    tok_rows = own_q.shape[0]
    features = own_q.shape[1]
    kv_features = own_k.shape[1]
    head_dim = HEAD_DIM
    head_count = features // head_dim
    kv_count = kv_features // head_dim
    group_size = head_count // kv_count
    band_reach = (WINDOW - 2) // tok_rows + 1
    band_len = (band_reach + 1) * tok_rows
    seq_len = tok_rows * lax.axis_size("seq")
    seq_pos = lax.axis_index("seq")
    attn_scale = 1.0 / math.sqrt(head_dim)
    positions = seq_pos * tok_rows + jnp.arange(tok_rows, dtype=jnp.int32)
    valid = ((positions < lengths[0]) & (loss_mask[0] == 1)).astype(jnp.float32)
    local_count = jnp.sum(valid)
    my_distance = distances[0].astype(jnp.float32)
    count_all = lax.psum(local_count, "seq")
    group_total = lax.psum(my_distance, "roll")
    advantage = (group_total / lax.axis_size("roll") - my_distance) / 64.0
    weight = advantage * valid * seq_len / (1.0 + count_all)
    arrived = lax.all_to_all(cotangent, "seq", split_axis=1, concat_axis=2, tiled=True)[0]
    dout = (arrived.astype(jnp.float32) * weight[:, None]).astype(jnp.bfloat16)
    kv_pair = jnp.stack([own_k, own_v])
    earlier = []
    for offset in range(1, band_reach + 1):
        earlier.append(passed_along(kv_pair, "seq", offset))
    ordered = earlier[::-1]
    band_k = jnp.concatenate([blk[0] for blk in ordered] + [own_k], 0)
    band_v = jnp.concatenate([blk[1] for blk in ordered] + [own_v], 0)
    key_pos = (seq_pos - band_reach) * tok_rows + jnp.arange(band_len, dtype=jnp.int32)
    pos_gap = positions[:, None] - key_pos[None, :]
    allowed = (pos_gap >= 0) & (pos_gap < WINDOW) & (key_pos[None, :] >= 0)
    gap_float = pos_gap.astype(jnp.float32)
    split_at = band_reach * tok_rows
    contract_rows = (((0,), (0,)), ((), ()))

    def head_step(head, carry):
        grad_q, own_dk, own_dv, part_k, part_v = carry
        column = head * head_dim
        kv_column = head // group_size * head_dim
        q_head = lax.dynamic_slice_in_dim(own_q, column, head_dim, 1)
        k_head = lax.dynamic_slice_in_dim(band_k, kv_column, head_dim, 1)
        v_head = lax.dynamic_slice_in_dim(band_v, kv_column, head_dim, 1)
        d_head = lax.dynamic_slice_in_dim(dout, column, head_dim, 1)
        slope = lax.dynamic_index_in_dim(slopes, head, keepdims=False)
        scores = (
            jnp.dot(q_head, k_head.T, preferred_element_type=jnp.float32) * attn_scale
            - slope * gap_float
        )
        masked = jnp.where(allowed, scores, -jnp.inf)
        row_max = jnp.max(masked, axis=1, keepdims=True)
        exp_terms = jnp.where(allowed, jnp.exp(masked - row_max), 0.0)
        probs = exp_terms / jnp.sum(exp_terms, axis=1, keepdims=True)
        probs_low = probs.astype(jnp.bfloat16)
        dprob = jnp.dot(d_head, v_head.T, preferred_element_type=jnp.float32)
        row_delta = jnp.sum(probs * dprob, axis=1, keepdims=True)
        dscore = (probs * (dprob - row_delta) * attn_scale).astype(jnp.bfloat16)
        head_dq = jnp.dot(dscore, k_head, preferred_element_type=jnp.float32).astype(jnp.bfloat16)
        band_dk = lax.dot_general(dscore, q_head, contract_rows, preferred_element_type=jnp.float32)
        band_dv = lax.dot_general(
            probs_low, d_head, contract_rows, preferred_element_type=jnp.float32
        )
        grad_q = lax.dynamic_update_slice_in_dim(grad_q, head_dq, column, 1)
        own_dk = lax.dynamic_update_slice_in_dim(
            own_dk,
            lax.dynamic_slice_in_dim(own_dk, kv_column, head_dim, 1) + band_dk[split_at:],
            kv_column,
            1,
        )
        own_dv = lax.dynamic_update_slice_in_dim(
            own_dv,
            lax.dynamic_slice_in_dim(own_dv, kv_column, head_dim, 1) + band_dv[split_at:],
            kv_column,
            1,
        )
        far_dk = band_dk[:split_at].reshape(band_reach, tok_rows, head_dim)
        far_dv = band_dv[:split_at].reshape(band_reach, tok_rows, head_dim)
        part_k = lax.dynamic_update_slice_in_dim(
            part_k, lax.dynamic_slice_in_dim(part_k, kv_column, head_dim, 2) + far_dk, kv_column, 2
        )
        part_v = lax.dynamic_update_slice_in_dim(
            part_v, lax.dynamic_slice_in_dim(part_v, kv_column, head_dim, 2) + far_dv, kv_column, 2
        )
        return (grad_q, own_dk, own_dv, part_k, part_v)

    start_carry = (
        jnp.zeros((tok_rows, features), jnp.bfloat16),
        jnp.zeros((tok_rows, kv_features), jnp.float32),
        jnp.zeros((tok_rows, kv_features), jnp.float32),
        jnp.zeros((band_reach, tok_rows, kv_features), jnp.float32),
        jnp.zeros((band_reach, tok_rows, kv_features), jnp.float32),
    )
    grad_q, total_k, total_v, part_k, part_v = lax.fori_loop(0, head_count, head_step, start_carry)
    part_k = part_k.astype(jnp.bfloat16)
    part_v = part_v.astype(jnp.bfloat16)
    for offset in range(1, band_reach + 1):
        outgoing = jnp.stack([part_k[band_reach - offset], part_v[band_reach - offset]])
        incoming = passed_along(outgoing, "seq", -offset)
        total_k = total_k + incoming[0].astype(jnp.float32)
        total_v = total_v + incoming[1].astype(jnp.float32)
    return (grad_q[None], total_k.astype(jnp.bfloat16)[None], total_v.astype(jnp.bfloat16)[None])


def solution(mesh):
    placed = (
        P("roll", "seq", None),
        P("roll", "seq", None),
        P("roll", "seq", None),
        P("roll", None, "seq"),
        P(),
        P("roll"),
        P("roll", "seq"),
        P("roll"),
    )
    return jax.shard_map(
        shards,
        mesh=mesh,
        in_specs=placed,
        out_specs=(P("roll", "seq", None), P("roll", "seq", None), P("roll", "seq", None)),
        check_vma=False,
    )
```

profile of v0, /device:TPU:19, one launch (start us, length us, event | category | flops | bytes accessed | tf_op | source)
XLA Modules:
  0.0 346.7 jit_solution(13123298232539514425)
XLA Ops:
  0.6 10.0 %copy.19 = bf16[1,4096,224]{2,0,1:T(2,128)(2,1)} copy(bf16[1,4096,224]{1,2,0:T(8,128)(2,1)} %param.13) | data formatting | bytes 3670016 | tf_op args[3]
  11.1 23.6 %reduce.2 = bf16[4096,224]{1,0:T(8,128)(2,1)S(1)} reduce(bf16[4096,1,224]{2,1,0:T(2,128)(2,1)} %bitcast.71, bf16[]{:T(256)} %broadcast.76), dimensions={1}, to_apply=%bitcast.53.reduce_sub_computation | reduce | bytes 3670018
  34.8 5.2 %reshape.80 = bf16[8,2,57344]{2,1,0:T(2,128)(2,1)} reshape(bf16[4096,224]{1,0:T(8,128)(2,1)S(1)} %reduce.2) | data formatting | bytes 3670016
  40.0 5.7 %all-to-all-start = ((bf16[8,2,57344]{2,1,0:T(2,128)(2,1)}), bf16[8,2,57344]{2,1,0:T(2,128)(2,1)S(1)}, u32[]{:S(2)}, u32[]{:S(2)}) async-start(bf16[8,2,57344]{2,1,0:T(2,128)(2,1)} %reshape.80), calls=%async_computation | async-start | bytes 3670016 | tf_op jit(solution)/shard_map/all_to_all | solution.py:41
  47.1 3.3 collective-permute-start.1
  50.4 1.9 collective-permute-start
  54.3 7.8 %psum.14 = f32[]{:T(128)} all-reduce(f32[]{:T(128)} %bitcast.7), channel_id=1, replica_groups=mesh['roll'=4,'seq'=8] {'roll'}, use_global_device_ids=true, to_apply=%region_0.0 | all-reduce | flops 1 | bytes 8 | tf_op jit(solution)/shard_map/psum | solution.py:38
  62.0 47.4 %psum.15 = f32[]{:T(128)} all-reduce(f32[]{:T(128)} %convert_reduce_fusion), channel_id=1, replica_groups=mesh['roll'=4,'seq'=8] {'seq'}, use_global_device_ids=true, to_apply=%region_2.0 | all-reduce | flops 1 | bytes 8 | tf_op jit(solution)/shard_map/psum | solution.py:37
  113.1 5.8 %reshape.81 = bf16[4096,1,224]{2,1,0:T(2,128)(2,1)} reshape(bf16[8,2,57344]{2,1,0:T(2,128)(2,1)S(1)} %all-to-all-done) | data formatting | bytes 3670016
  118.9 10.1 %copy.20 = bf16[1,4096,224]{1,2,0:T(8,128)(2,1)S(1)} copy(bf16[1,4096,224]{2,0,1:T(2,128)(2,1)} %bitcast.72) | data formatting | bytes 3670016 | tf_op jit(solution)/shard_map/all_to_all | solution.py:41
  129.5 3.3 copy.24
  132.7 2.1 copy.21
  134.9 1.8 fusion.30
  138.3 186.0 %while.25 = (s32[]{:T(128)}, bf16[512,1792]{1,0:T(8,128)(2,1)}, f32[512,256]{1,0:T(8,128)S(1)}, f32[512,256]{1,0:T(8,128)S(1)}, f32[2,512,256]{2,1,0:T(8,128)S(1...) while((s32[]{:T(128)}, bf16[512,1792]{1,0:T(8,128)(2,1)}, ...), condition=%wide.region_7.8_spmd.clone.clone, body=%wide.region_3.7_spmd.clone.clone.sunk | while | flops 1033828864 | bytes 46446556 | solution.py:113
  138.8 3.3 fusion.59
  143.5 2.8 multiply_reduce_fusion.2
  152.1 3.3 fusion.59
  156.8 2.8 multiply_reduce_fusion.2
  165.4 3.3 fusion.59
  170.0 2.8 multiply_reduce_fusion.2
  178.6 3.3 fusion.59
  183.3 2.8 multiply_reduce_fusion.2
  191.9 3.3 fusion.59
  196.6 2.8 multiply_reduce_fusion.2
  205.2 3.3 fusion.59
  209.8 2.8 multiply_reduce_fusion.2
  218.4 3.3 fusion.59
  223.1 2.8 multiply_reduce_fusion.2
  231.7 3.3 fusion.59
  236.3 2.8 multiply_reduce_fusion.2
  239.6 1.6 fusion.62
  245.0 3.3 fusion.59
  249.7 2.8 multiply_reduce_fusion.2
  252.9 1.6 fusion.62
  258.3 3.3 fusion.59
  263.0 2.8 multiply_reduce_fusion.2
  271.7 3.3 fusion.59
  276.3 2.8 multiply_reduce_fusion.2
  285.0 3.3 fusion.59
  289.6 2.8 multiply_reduce_fusion.2
  298.3 3.3 fusion.59
  303.0 2.8 multiply_reduce_fusion.2
  311.6 3.3 fusion.59
  316.3 2.8 multiply_reduce_fusion.2
  324.6 1.9 collective-permute-start.3
  326.6 2.1 collective-permute-start.2
  328.7 11.2 %collective-permute-done.3 = bf16[2,512,256]{2,1,0:T(8,128)(2,1)S(1)} collective-permute-done((bf16[2,512,256]{2,1,0:T(8,128)(2,1)S(1)}, bf16[2,512,256]{2,1,0:T(8,128)(2,1)S(1)}, u32[]{:S(2)}, u32[]{:S(2)}) %collective-permute-start.3) | collective-permute-done | bytes 524320 | tf_op jit(solution)/shard_map/ppermute | solution.py:14
  339.9 5.9 %collective-permute-done.2 = bf16[2,512,256]{2,1,0:T(8,128)(2,1)S(1)} collective-permute-done((bf16[2,512,256]{2,1,0:T(8,128)(2,1)S(1)}, bf16[2,512,256]{2,1,0:T(8,128)(2,1)S(1)}, u32[]{:S(2)}, u32[]{:S(2)}) %collective-permute-start.2) | collective-permute-done | bytes 524320 | tf_op jit(solution)/shard_map/ppermute | solution.py:14
  (230 shorter events, 104.8 us)
Async XLA Ops:
  34.7 10.9 %copy-start.1 = (bf16[1,512,256]{2,1,0:T(8,128)(2,1)S(1)}, bf16[1,512,256]{2,1,0:T(8,128)(2,1)}, u32[]{:S(2)}) copy-start(bf16[1,512,256]{2,1,0:T(8,128)(2,1)} %param.11) | copy-start | bytes 786436
  34.8 11.6 %copy-start.2 = (bf16[1,512,256]{2,1,0:T(8,128)(2,1)S(1)}, bf16[1,512,256]{2,1,0:T(8,128)(2,1)}, u32[]{:S(2)}) copy-start(bf16[1,512,256]{2,1,0:T(8,128)(2,1)} %param.12) | copy-start | bytes 786436
  40.0 13.7 %copy-start.4 = (s32[1,512]{1,0:T(1,128)S(1)}, s32[1,512]{1,0:T(1,128)}, u32[]{:S(2)}) copy-start(s32[1,512]{1,0:T(1,128)} %param.16) | copy-start | bytes 6148
  40.0 73.2 %all-to-all-start = ((bf16[8,2,57344]{2,1,0:T(2,128)(2,1)}), bf16[8,2,57344]{2,1,0:T(2,128)(2,1)S(1)}, u32[]{:S(2)}, u32[]{:S(2)}) async-start(bf16[8,2,57344]{2,1,0:T(2,128)(2,1)} %reshape.80), calls=%async_computation | async-start | bytes 3670016 | tf_op jit(solution)/shard_map/all_to_all | solution.py:41
  47.1 63.7 %collective-permute-start.1 = (bf16[2,512,256]{2,1,0:T(8,128)(2,1)}, bf16[2,512,256]{2,1,0:T(8,128)(2,1)}, u32[]{:S(2)}, u32[]{:S(2)}) collective-permute-start(bf16[2,512,256]{2,1,0:T(8,128)(2,1)} %constant_dynamic-update-slice_fusion), channel_id=1, source_target_pairs={{0,1},{1,2},{2,3},{3,4},{4,5},{5,6},{6,7},{8,9},{9,10},{10,11},{11... | collective-permute-start | bytes 1572872 | tf_op jit(solution)/shard_map/ppermute | solution.py:14
  50.4 61.4 %collective-permute-start = (bf16[2,512,256]{2,1,0:T(8,128)(2,1)}, bf16[2,512,256]{2,1,0:T(8,128)(2,1)S(1)}, u32[]{:S(2)}, u32[]{:S(2)}) collective-permute-start(bf16[2,512,256]{2,1,0:T(8,128)(2,1)} %constant_dynamic-update-slice_fusion), channel_id=1, source_target_pairs={{0,2},{1,3},{2,4},{3,5},{4,6},{5,7},{8,10},{9,11},{10,12},{11,13},... | collective-permute-start | bytes 1572872 | tf_op jit(solution)/shard_map/ppermute | solution.py:14
  136.7 1.6 copy-start.5
  142.1 1.4 copy-start.3
  146.7 3.2 copy-start
  155.4 1.4 copy-start.3
  160.0 3.2 copy-start
  168.6 1.4 copy-start.3
  173.2 3.2 copy-start
  181.9 1.4 copy-start.3
  186.5 3.2 copy-start
  195.2 1.4 copy-start.3
  199.8 3.2 copy-start
  208.4 1.4 copy-start.3
  213.0 3.2 copy-start
  221.7 1.4 copy-start.3
  226.3 3.2 copy-start
  235.0 1.4 copy-start.3
  239.6 3.2 copy-start
  248.3 1.4 copy-start.3
  252.9 3.2 copy-start
  261.6 1.4 copy-start.3
  266.2 3.2 copy-start
  274.9 1.4 copy-start.3
  279.5 3.2 copy-start
  288.3 1.4 copy-start.3
  292.8 3.2 copy-start
  301.6 1.4 copy-start.3
  306.2 3.2 copy-start
  314.9 1.4 copy-start.3
  319.5 3.2 copy-start
  324.6 15.3 %collective-permute-start.3 = (bf16[2,512,256]{2,1,0:T(8,128)(2,1)S(1)}, bf16[2,512,256]{2,1,0:T(8,128)(2,1)S(1)}, u32[]{:S(2)}, u32[]{:S(2)}) collective-permute-start(bf16[2,512,256]{2,1,0:T(8,128)(2,1)S(1)} %pad_maximum_fusion.3), channel_id=1, source_target_pairs={{2,0},{3,1},{4,2},{5,3},{6,4},{7,5},{10,8},{11,9},{12,10},{13,11},... | collective-permute-start | bytes 1572872 | tf_op jit(solution)/shard_map/ppermute | solution.py:14
  326.6 19.2 %collective-permute-start.2 = (bf16[2,512,256]{2,1,0:T(8,128)(2,1)S(1)}, bf16[2,512,256]{2,1,0:T(8,128)(2,1)S(1)}, u32[]{:S(2)}, u32[]{:S(2)}) collective-permute-start(bf16[2,512,256]{2,1,0:T(8,128)(2,1)S(1)} %pad_maximum_fusion.2), channel_id=1, source_target_pairs={{1,0},{2,1},{3,2},{4,3},{5,4},{6,5},{7,6},{9,8},{10,9},{11,10},{12... | collective-permute-start | bytes 1572872 | tf_op jit(solution)/shard_map/ppermute | solution.py:14
where the time goes:
time: 349 us; the launch traced here: 347 us
  matrix products  146 us (42%)
  other arithmetic  58.4 us (17%)
  blocking collectives  55.2 us (16%)
  local copies, waits for them, and re-layouts  50.5 us (14%)
  waiting for transfers between devices  17.1 us (5%)
  starting transfers between devices  14.9 us (4%)
    psum x1, blocking collectives, shards(): count_all = lax.psum(local_count, 'seq')  47.4 us
    dot_general x14, matrix products, head_step(): jnp.dot(q_head, k_head.T, preferred_element_type=jnp.float32) * attn_scale  45.8 us
    dot_general x14, matrix products, head_step(): dprob = jnp.dot(d_head, v_head.T, preferred_element_type=jnp.float32)  38.8 us
    unnamed x14, local copies, waits for them, and re-layouts  25.4 us
    unnamed x1, other arithmetic  23.6 us
    dot_general x14, matrix products, head_step(): lax.dot_general(probs_low, d_head, contract_rows, preferred_element_type=...  22.3 us
    dot_general x14, matrix products, head_step(): lax.dot_general(dscore, q_head, contract_rows, preferred_element_type=jnp...  21.3 us
    reduce_sum x14, other arithmetic, head_step(): probs = exp_terms / jnp.sum(exp_terms, axis=1, keepdims=True)  19.1 us
  transfers between devices with their start and end apart: 5, of which 2 were waited for; matrix products, arithmetic and copies ran while one was open for 1% of the time, Pallas kernels for 0%

commit v1 on v0

--- a/solution.py
+++ b/solution.py
@@ -6,6 +6,29 @@
 
 HEAD_DIM = 128
 WINDOW = 1024
+
+
+def split_up(x, dim, length):
+    shape = x.shape
+    blocks = x.reshape(*shape[:dim], length, shape[dim] // length, *shape[dim + 1 :])
+    return jnp.moveaxis(blocks, dim, 0)
+
+
+def in_order(blocks, dim):
+    blocks = jnp.moveaxis(blocks, 0, dim)
+    dims = blocks.shape
+    return blocks.reshape(*dims[:dim], dims[dim] * dims[dim + 1], *dims[dim + 2 :])
+
+
+def exchange_in_pairs(x, axis, split_dim, concat_dim):
+    length, here = (lax.axis_size(axis), lax.axis_index(axis))
+    blocks = split_up(x, split_dim, length)
+    outs = [blocks[here]]
+    for step in range(1, length):
+        sent = blocks[here ^ step]
+        outs.append(lax.ppermute(sent, axis, [(i, i ^ step) for i in range(length)]))
+    blocks = jnp.stack(outs)[here ^ jnp.arange(length)]
+    return in_order(blocks, concat_dim)
 
 
 def passed_along(value, axis, steps):
@@ -38,7 +61,7 @@
     group_total = lax.psum(my_distance, "roll")
     advantage = (group_total / lax.axis_size("roll") - my_distance) / 64.0
     weight = advantage * valid * seq_len / (1.0 + count_all)
-    arrived = lax.all_to_all(cotangent, "seq", split_axis=1, concat_axis=2, tiled=True)[0]
+    arrived = exchange_in_pairs(cotangent, "seq", 1, 2)[0]
     dout = (arrived.astype(jnp.float32) * weight[:, None]).astype(jnp.bfloat16)
     kv_pair = jnp.stack([own_k, own_v])
     earlier = []

time: 349 us -> 316 us (0.905)
  blocking collectives: 55.2 us -> 19.5 us
  waiting for transfers between devices: 17.1 us -> 50.6 us
  other arithmetic: 58.4 us -> 34.9 us
  local copies, waits for them, and re-layouts: 50.5 us -> 35.2 us
  starting transfers between devices: 14.9 us -> 20.7 us
    psum x1, blocking collectives: 47.4 us -> 12 us  [shards(): count_all = lax.psum(local_count, 'seq')]
    ppermute x0 -> x7, waiting for transfers between devices: none -> 34.2 us  [exchange_in_pairs(): lax.ppermute(sent, axis, [(i, i ^ step) for i in range(length)])]
    unnamed x1 -> x0, other arithmetic: 23.6 us -> none
    unnamed x14 -> x30, local copies, waits for them, and re-layouts: 25.4 us -> 13.6 us
    ppermute x0 -> x7, starting transfers between devices: none -> 10.3 us  [exchange_in_pairs(): lax.ppermute(sent, axis, [(i, i ^ step) for i in range(length)])]
    all_to_all x1 -> x0, local copies, waits for them, and re-layouts: 10.1 us -> none  [shards(): lax.all_to_all(cotangent, 'seq', split_axis=1, concat_axis=2, tiled=True)[0]]
    all_to_all x1 -> x0, starting transfers between devices: 5.66 us -> none  [shards(): lax.all_to_all(cotangent, 'seq', split_axis=1, concat_axis=2, tiled=True)[0]]
    dynamic_slice x0 -> x1, local copies, waits for them, and re-layouts: none -> 4.6 us  [exchange_in_pairs(): sent = blocks[here ^ step]]
  transfers between devices with their start and end apart: 5 -> 11, of which waited for: 2 -> 6; matrix products, arithmetic and copies ran while one was open for 1% -> 7% of each run, Pallas kernels for 0% -> 0%
where the time goes in v1:
time: 316 us; the launch traced here: 312 us
  matrix products  146 us (46%)
  waiting for transfers between devices  50.6 us (16%)
  local copies, waits for them, and re-layouts  35.2 us (11%)
  other arithmetic  34.9 us (11%)
  starting transfers between devices  20.7 us (7%)
  blocking collectives  19.5 us (6%)
  between operations  3.53 us (1%)
    dot_general x14, matrix products, head_step(): jnp.dot(q_head, k_head.T, preferred_element_type=jnp.float32) * attn_scale  45.8 us
    dot_general x14, matrix products, head_step(): dprob = jnp.dot(d_head, v_head.T, preferred_element_type=jnp.float32)  38.8 us
    ppermute x7, waiting for transfers between devices, exchange_in_pairs(): lax.ppermute(sent, axis, [(i, i ^ step) for i in range(length)])  34.2 us
    dot_general x14, matrix products, head_step(): lax.dot_general(dscore, q_head, contract_rows, preferred_element_type=jnp...  22.2 us
    dot_general x14, matrix products, head_step(): lax.dot_general(probs_low, d_head, contract_rows, preferred_element_type=...  21.3 us
    reduce_sum x14, other arithmetic, head_step(): probs = exp_terms / jnp.sum(exp_terms, axis=1, keepdims=True)  19.1 us
    dot_general x14, matrix products, head_step(): jnp.dot(dscore, k_head, preferred_element_type=jnp.float32)  17.4 us
    ppermute x4, waiting for transfers between devices, passed_along(): lax.ppermute(value, axis, [(source, source + steps) for source in range(l...  16.4 us
  transfers between devices with their start and end apart: 11, of which 6 were waited for; matrix products, arithmetic and copies ran while one was open for 7% of the time, Pallas kernels for 0%

profile of v1, /device:TPU:19, one launch (start us, length us, event | category | flops | bytes accessed | tf_op | source)
XLA Modules:
  0.0 311.6 jit_solution(8846768048664474882)
XLA Ops:
  4.0 3.8 %collective-permute-start.1 = (bf16[2,512,256]{2,1,0:T(8,128)(2,1)}, bf16[2,512,256]{2,1,0:T(8,128)(2,1)}, u32[]{:S(2)}, u32[]{:S(2)}) collective-permute-start(bf16[2,512,256]{2,1,0:T(8,128)(2,1)} %constant_dynamic-update-slice_fusion), channel_id=1, source_target_pairs={{0,1},{1,2},{2,3},{3,4},{4,5},{5,6},{6,7},{8,9},{9,10},{10,11},{11... | collective-permute-start | bytes 1572872 | tf_op jit(solution)/shard_map/ppermute | solution.py:37
  7.8 1.9 collective-permute-start
  9.7 2.3 copy.37
  12.0 4.6 %constant_dynamic-slice_fusion = (bf16[1,1,512,224]{2,0,3,1:T(2,128)(2,1)}, bf16[1,1,512,224]{2,0,3,1:T(2,128)(2,1)S(1)}, bf16[1,1,512,224]{2,0,3,1:T(2,128)(2,1...) fusion(bf16[8,1,512,224]{2,0,3,1:T(8,128)(2,1)S(1)} %bitcast.12, ...), kind=kLoop, calls=%fused_computation.89 | loop fusion | bytes 3670048 | tf_op jit(solution)/shard_map/dynamic_slice | solution.py:28
  19.2 1.8 collective-permute-start.4
  24.0 7.5 %psum.14 = f32[]{:T(128)} all-reduce(f32[]{:T(128)} %bitcast.24), channel_id=1, replica_groups=mesh['roll'=4,'seq'=8] {'roll'}, use_global_device_ids=true, to_apply=%region_0.0 | all-reduce | flops 1 | bytes 8 | tf_op jit(solution)/shard_map/psum | solution.py:61
  31.5 12.0 %psum.15 = f32[]{:T(128)} all-reduce(f32[]{:T(128)} %convert_reduce_fusion), channel_id=1, replica_groups=mesh['roll'=4,'seq'=8] {'seq'}, use_global_device_ids=true, to_apply=%region_2.0 | all-reduce | flops 1 | bytes 8 | tf_op jit(solution)/shard_map/psum | solution.py:60
  48.0 5.4 %collective-permute-start.5 = (bf16[1,512,224]{1,2,0:T(8,128)(2,1)S(1)}, bf16[1,512,224]{1,2,0:T(8,128)(2,1)S(1)}, u32[]{:S(2)}, u32[]{:S(2)}) collective-permute-start(bf16[1,512,224]{1,2,0:T(8,128)(2,1)S(1)} %bitcast.134), channel_id=1, source_target_pairs={{0,4},{1,5},{2,6},{3,7},{4,0},{5,1},{6,2},{7,3},{8,12},{9,13},{10,... | collective-permute-start | bytes 688136 | tf_op jit(solution)/shard_map/ppermute | solution.py:29
  56.0 14.8 %collective-permute-done.5 = bf16[1,512,224]{1,2,0:T(8,128)(2,1)S(1)} collective-permute-done((bf16[1,512,224]{1,2,0:T(8,128)(2,1)S(1)}, bf16[1,512,224]{1,2,0:T(8,128)(2,1)S(1)}, u32[]{:S(2)}, u32[]{:S(2)}) %collective-permute-start.5) | collective-permute-done | bytes 229408 | tf_op jit(solution)/shard_map/ppermute | solution.py:29
  70.8 2.1 collective-permute-start.8
  72.9 2.9 collective-permute-done.6
  75.8 11.6 %collective-permute-done.7 = bf16[1,512,224]{1,2,0:T(8,128)(2,1)S(1)} collective-permute-done((bf16[1,512,224]{1,2,0:T(8,128)(2,1)S(1)}, bf16[1,512,224]{1,2,0:T(8,128)(2,1)S(1)}, u32[]{:S(2)}, u32[]{:S(2)}) %collective-permute-start.7) | collective-permute-done | bytes 229408 | tf_op jit(solution)/shard_map/ppermute | solution.py:29
  87.5 4.9 %collective-permute-done.8 = bf16[1,512,224]{1,2,0:T(8,128)(2,1)S(1)} collective-permute-done((bf16[1,512,224]{1,2,0:T(8,128)(2,1)S(1)}, bf16[1,512,224]{1,2,0:T(8,128)(2,1)S(1)}, u32[]{:S(2)}, u32[]{:S(2)}) %collective-permute-start.8) | collective-permute-done | bytes 229408 | tf_op jit(solution)/shard_map/ppermute | solution.py:29
  93.7 2.2 gather_fusion
  96.3 1.8 fusion.30
  103.2 186.0 %while.25 = (s32[]{:T(128)}, bf16[512,1792]{1,0:T(8,128)(2,1)}, f32[512,256]{1,0:T(8,128)S(1)}, f32[512,256]{1,0:T(8,128)S(1)}, f32[2,512,256]{2,1,0:T(8,128)S(1...) while((s32[]{:T(128)}, bf16[512,1792]{1,0:T(8,128)(2,1)}, ...), condition=%wide.region_7.8_spmd.clone.clone, body=%wide.region_3.7_spmd.clone.clone.sunk | while | flops 1033828864 | bytes 46446556 | solution.py:136
  103.8 3.3 %fusion.60 = (f32[512]{0:T(512)S(1)}, f32[512,1536]{1,0:T(8,128)S(1)}) fusion(f32[]{:T(128)} %bitcast.117, bf16[1536,256]{1,0:T(8,128)(2,1)} %get-tuple-element.633, s32[]{:T(128)S(6)} %select_n.143, bf16[512,1792]{1,0:T(8,128)(2,1)} %get-tuple-element.632, s32[]{:T(128)S(6)} %select_n.141, pred[1536]{0:T(1024)(128)(4,1)S(1)} %get-tuple-element.639, ...), kind=kOutput, calls=%fused_computation.99.clone.1 | convolution fusion | flops 209976832 | bytes 3682312 | tf_op jit(solution)/shard_map/while/body/eval_jaxpr/dot_general | solution.py:90
  108.5 2.8 multiply_reduce_fusion.2
  117.1 3.3 %fusion.60 = (f32[512]{0:T(512)S(1)}, f32[512,1536]{1,0:T(8,128)S(1)}) fusion(f32[]{:T(128)} %bitcast.117, bf16[1536,256]{1,0:T(8,128)(2,1)} %get-tuple-element.633, s32[]{:T(128)S(6)} %select_n.143, bf16[512,1792]{1,0:T(8,128)(2,1)} %get-tuple-element.632, s32[]{:T(128)S(6)} %select_n.141, pred[1536]{0:T(1024)(128)(4,1)S(1)} %get-tuple-element.639, ...), kind=kOutput, calls=%fused_computation.99.clone.1 | convolution fusion | flops 209976832 | bytes 3682312 | tf_op jit(solution)/shard_map/while/body/eval_jaxpr/dot_general | solution.py:90
  121.7 2.8 multiply_reduce_fusion.2
  130.3 3.3 %fusion.60 = (f32[512]{0:T(512)S(1)}, f32[512,1536]{1,0:T(8,128)S(1)}) fusion(f32[]{:T(128)} %bitcast.117, bf16[1536,256]{1,0:T(8,128)(2,1)} %get-tuple-element.633, s32[]{:T(128)S(6)} %select_n.143, bf16[512,1792]{1,0:T(8,128)(2,1)} %get-tuple-element.632, s32[]{:T(128)S(6)} %select_n.141, pred[1536]{0:T(1024)(128)(4,1)S(1)} %get-tuple-element.639, ...), kind=kOutput, calls=%fused_computation.99.clone.1 | convolution fusion | flops 209976832 | bytes 3682312 | tf_op jit(solution)/shard_map/while/body/eval_jaxpr/dot_general | solution.py:90
  135.0 2.8 multiply_reduce_fusion.2
  143.6 3.3 %fusion.60 = (f32[512]{0:T(512)S(1)}, f32[512,1536]{1,0:T(8,128)S(1)}) fusion(f32[]{:T(128)} %bitcast.117, bf16[1536,256]{1,0:T(8,128)(2,1)} %get-tuple-element.633, s32[]{:T(128)S(6)} %select_n.143, bf16[512,1792]{1,0:T(8,128)(2,1)} %get-tuple-element.632, s32[]{:T(128)S(6)} %select_n.141, pred[1536]{0:T(1024)(128)(4,1)S(1)} %get-tuple-element.639, ...), kind=kOutput, calls=%fused_computation.99.clone.1 | convolution fusion | flops 209976832 | bytes 3682312 | tf_op jit(solution)/shard_map/while/body/eval_jaxpr/dot_general | solution.py:90
  148.2 2.8 multiply_reduce_fusion.2
  156.8 3.3 %fusion.60 = (f32[512]{0:T(512)S(1)}, f32[512,1536]{1,0:T(8,128)S(1)}) fusion(f32[]{:T(128)} %bitcast.117, bf16[1536,256]{1,0:T(8,128)(2,1)} %get-tuple-element.633, s32[]{:T(128)S(6)} %select_n.143, bf16[512,1792]{1,0:T(8,128)(2,1)} %get-tuple-element.632, s32[]{:T(128)S(6)} %select_n.141, pred[1536]{0:T(1024)(128)(4,1)S(1)} %get-tuple-element.639, ...), kind=kOutput, calls=%fused_computation.99.clone.1 | convolution fusion | flops 209976832 | bytes 3682312 | tf_op jit(solution)/shard_map/while/body/eval_jaxpr/dot_general | solution.py:90
  161.5 2.8 multiply_reduce_fusion.2
  170.1 3.3 %fusion.60 = (f32[512]{0:T(512)S(1)}, f32[512,1536]{1,0:T(8,128)S(1)}) fusion(f32[]{:T(128)} %bitcast.117, bf16[1536,256]{1,0:T(8,128)(2,1)} %get-tuple-element.633, s32[]{:T(128)S(6)} %select_n.143, bf16[512,1792]{1,0:T(8,128)(2,1)} %get-tuple-element.632, s32[]{:T(128)S(6)} %select_n.141, pred[1536]{0:T(1024)(128)(4,1)S(1)} %get-tuple-element.639, ...), kind=kOutput, calls=%fused_computation.99.clone.1 | convolution fusion | flops 209976832 | bytes 3682312 | tf_op jit(solution)/shard_map/while/body/eval_jaxpr/dot_general | solution.py:90
  174.8 2.8 multiply_reduce_fusion.2
  183.4 3.3 %fusion.60 = (f32[512]{0:T(512)S(1)}, f32[512,1536]{1,0:T(8,128)S(1)}) fusion(f32[]{:T(128)} %bitcast.117, bf16[1536,256]{1,0:T(8,128)(2,1)} %get-tuple-element.633, s32[]{:T(128)S(6)} %select_n.143, bf16[512,1792]{1,0:T(8,128)(2,1)} %get-tuple-element.632, s32[]{:T(128)S(6)} %select_n.141, pred[1536]{0:T(1024)(128)(4,1)S(1)} %get-tuple-element.639, ...), kind=kOutput, calls=%fused_computation.99.clone.1 | convolution fusion | flops 209976832 | bytes 3682312 | tf_op jit(solution)/shard_map/while/body/eval_jaxpr/dot_general | solution.py:90
  188.0 2.8 multiply_reduce_fusion.2
  196.6 3.3 %fusion.60 = (f32[512]{0:T(512)S(1)}, f32[512,1536]{1,0:T(8,128)S(1)}) fusion(f32[]{:T(128)} %bitcast.117, bf16[1536,256]{1,0:T(8,128)(2,1)} %get-tuple-element.633, s32[]{:T(128)S(6)} %select_n.143, bf16[512,1792]{1,0:T(8,128)(2,1)} %get-tuple-element.632, s32[]{:T(128)S(6)} %select_n.141, pred[1536]{0:T(1024)(128)(4,1)S(1)} %get-tuple-element.639, ...), kind=kOutput, calls=%fused_computation.99.clone.1 | convolution fusion | flops 209976832 | bytes 3682312 | tf_op jit(solution)/shard_map/while/body/eval_jaxpr/dot_general | solution.py:90
  201.3 2.8 multiply_reduce_fusion.2
  209.9 3.3 %fusion.60 = (f32[512]{0:T(512)S(1)}, f32[512,1536]{1,0:T(8,128)S(1)}) fusion(f32[]{:T(128)} %bitcast.117, bf16[1536,256]{1,0:T(8,128)(2,1)} %get-tuple-element.633, s32[]{:T(128)S(6)} %select_n.143, bf16[512,1792]{1,0:T(8,128)(2,1)} %get-tuple-element.632, s32[]{:T(128)S(6)} %select_n.141, pred[1536]{0:T(1024)(128)(4,1)S(1)} %get-tuple-element.639, ...), kind=kOutput, calls=%fused_computation.99.clone.1 | convolution fusion | flops 209976832 | bytes 3682312 | tf_op jit(solution)/shard_map/while/body/eval_jaxpr/dot_general | solution.py:90
  214.6 2.8 multiply_reduce_fusion.2
  223.2 3.3 %fusion.60 = (f32[512]{0:T(512)S(1)}, f32[512,1536]{1,0:T(8,128)S(1)}) fusion(f32[]{:T(128)} %bitcast.117, bf16[1536,256]{1,0:T(8,128)(2,1)} %get-tuple-element.633, s32[]{:T(128)S(6)} %select_n.143, bf16[512,1792]{1,0:T(8,128)(2,1)} %get-tuple-element.632, s32[]{:T(128)S(6)} %select_n.141, pred[1536]{0:T(1024)(128)(4,1)S(1)} %get-tuple-element.639, ...), kind=kOutput, calls=%fused_computation.99.clone.1 | convolution fusion | flops 209976832 | bytes 3682312 | tf_op jit(solution)/shard_map/while/body/eval_jaxpr/dot_general | solution.py:90
  227.9 2.8 multiply_reduce_fusion.2
  236.6 3.3 %fusion.60 = (f32[512]{0:T(512)S(1)}, f32[512,1536]{1,0:T(8,128)S(1)}) fusion(f32[]{:T(128)} %bitcast.117, bf16[1536,256]{1,0:T(8,128)(2,1)} %get-tuple-element.633, s32[]{:T(128)S(6)} %select_n.143, bf16[512,1792]{1,0:T(8,128)(2,1)} %get-tuple-element.632, s32[]{:T(128)S(6)} %select_n.141, pred[1536]{0:T(1024)(128)(4,1)S(1)} %get-tuple-element.639, ...), kind=kOutput, calls=%fused_computation.99.clone.1 | convolution fusion | flops 209976832 | bytes 3682312 | tf_op jit(solution)/shard_map/while/body/eval_jaxpr/dot_general | solution.py:90
  241.2 2.8 multiply_reduce_fusion.2
  249.9 3.3 %fusion.60 = (f32[512]{0:T(512)S(1)}, f32[512,1536]{1,0:T(8,128)S(1)}) fusion(f32[]{:T(128)} %bitcast.117, bf16[1536,256]{1,0:T(8,128)(2,1)} %get-tuple-element.633, s32[]{:T(128)S(6)} %select_n.143, bf16[512,1792]{1,0:T(8,128)(2,1)} %get-tuple-element.632, s32[]{:T(128)S(6)} %select_n.141, pred[1536]{0:T(1024)(128)(4,1)S(1)} %get-tuple-element.639, ...), kind=kOutput, calls=%fused_computation.99.clone.1 | convolution fusion | flops 209976832 | bytes 3682312 | tf_op jit(solution)/shard_map/while/body/eval_jaxpr/dot_general | solution.py:90
  254.5 2.8 multiply_reduce_fusion.2
  263.2 3.3 %fusion.60 = (f32[512]{0:T(512)S(1)}, f32[512,1536]{1,0:T(8,128)S(1)}) fusion(f32[]{:T(128)} %bitcast.117, bf16[1536,256]{1,0:T(8,128)(2,1)} %get-tuple-element.633, s32[]{:T(128)S(6)} %select_n.143, bf16[512,1792]{1,0:T(8,128)(2,1)} %get-tuple-element.632, s32[]{:T(128)S(6)} %select_n.141, pred[1536]{0:T(1024)(128)(4,1)S(1)} %get-tuple-element.639, ...), kind=kOutput, calls=%fused_computation.99.clone.1 | convolution fusion | flops 209976832 | bytes 3682312 | tf_op jit(solution)/shard_map/while/body/eval_jaxpr/dot_general | solution.py:90
  267.9 2.8 multiply_reduce_fusion.2
  276.5 3.3 %fusion.60 = (f32[512]{0:T(512)S(1)}, f32[512,1536]{1,0:T(8,128)S(1)}) fusion(f32[]{:T(128)} %bitcast.117, bf16[1536,256]{1,0:T(8,128)(2,1)} %get-tuple-element.633, s32[]{:T(128)S(6)} %select_n.143, bf16[512,1792]{1,0:T(8,128)(2,1)} %get-tuple-element.632, s32[]{:T(128)S(6)} %select_n.141, pred[1536]{0:T(1024)(128)(4,1)S(1)} %get-tuple-element.639, ...), kind=kOutput, calls=%fused_computation.99.clone.1 | convolution fusion | flops 209976832 | bytes 3682312 | tf_op jit(solution)/shard_map/while/body/eval_jaxpr/dot_general | solution.py:90
  281.2 2.8 multiply_reduce_fusion.2
  289.5 2.1 collective-permute-start.10
  291.7 2.6 collective-permute-start.9
  294.3 10.3 %collective-permute-done.10 = bf16[2,512,256]{2,1,0:T(8,128)(2,1)S(1)} collective-permute-done((bf16[2,512,256]{2,1,0:T(8,128)(2,1)S(1)}, bf16[2,512,256]{2,1,0:T(8,128)(2,1)S(1)}, u32[]{:S(2)}, u32[]{:S(2)}) %collective-permute-start.10) | collective-permute-done | bytes 524320 | tf_op jit(solution)/shard_map/ppermute | solution.py:37
  304.6 6.1 %collective-permute-done.9 = bf16[2,512,256]{2,1,0:T(8,128)(2,1)S(1)} collective-permute-done((bf16[2,512,256]{2,1,0:T(8,128)(2,1)S(1)}, bf16[2,512,256]{2,1,0:T(8,128)(2,1)S(1)}, u32[]{:S(2)}, u32[]{:S(2)}) %collective-permute-start.9) | collective-permute-done | bytes 524320 | tf_op jit(solution)/shard_map/ppermute | solution.py:37
  (260 shorter events, 121.2 us)
Async XLA Ops:
  4.0 94.2 %collective-permute-start.1 = (bf16[2,512,256]{2,1,0:T(8,128)(2,1)}, bf16[2,512,256]{2,1,0:T(8,128)(2,1)}, u32[]{:S(2)}, u32[]{:S(2)}) collective-permute-start(bf16[2,512,256]{2,1,0:T(8,128)(2,1)} %constant_dynamic-update-slice_fusion), channel_id=1, source_target_pairs={{0,1},{1,2},{2,3},{3,4},{4,5},{5,6},{6,7},{8,9},{9,10},{10,11},{11... | collective-permute-start | bytes 1572872 | tf_op jit(solution)/shard_map/ppermute | solution.py:37
  7.8 91.5 %collective-permute-start = (bf16[2,512,256]{2,1,0:T(8,128)(2,1)}, bf16[2,512,256]{2,1,0:T(8,128)(2,1)}, u32[]{:S(2)}, u32[]{:S(2)}) collective-permute-start(bf16[2,512,256]{2,1,0:T(8,128)(2,1)} %constant_dynamic-update-slice_fusion), channel_id=1, source_target_pairs={{0,2},{1,3},{2,4},{3,5},{4,6},{5,7},{8,10},{9,11},{10,12},{11,13},... | collective-permute-start | bytes 1572872 | tf_op jit(solution)/shard_map/ppermute | solution.py:37
  16.6 5.0 %copy-start.7 = (s32[1,512]{1,0:T(1,128)S(1)}, s32[1,512]{1,0:T(1,128)}, u32[]{:S(2)}) copy-start(s32[1,512]{1,0:T(1,128)} %param.16) | copy-start | bytes 6148
  17.4 30.6 %collective-permute-start.2 = (bf16[1,512,224]{1,2,0:T(8,128)(2,1)}, bf16[1,512,224]{1,2,0:T(8,128)(2,1)}, u32[]{:S(2)}, u32[]{:S(2)}) collective-permute-start(bf16[1,512,224]{1,2,0:T(8,128)(2,1)} %bitcast.109), channel_id=1, source_target_pairs={{0,1},{1,0},{2,3},{3,2},{4,5},{5,4},{6,7},{7,6},{8,9},{9,8},{10,11... | collective-permute-start | bytes 688136 | tf_op jit(solution)/shard_map/ppermute | solution.py:29
  18.5 35.8 %collective-permute-start.3 = (bf16[1,512,224]{1,2,0:T(8,128)(2,1)}, bf16[1,512,224]{1,2,0:T(8,128)(2,1)}, u32[]{:S(2)}, u32[]{:S(2)}) collective-permute-start(bf16[1,512,224]{1,2,0:T(8,128)(2,1)} %bitcast.108), channel_id=1, source_target_pairs={{0,2},{1,3},{2,0},{3,1},{4,6},{5,7},{6,4},{7,5},{8,10},{9,11},{10,... | collective-permute-start | bytes 688136 | tf_op jit(solution)/shard_map/ppermute | solution.py:29
  19.2 36.7 %collective-permute-start.4 = (bf16[1,512,224]{1,2,0:T(8,128)(2,1)}, bf16[1,512,224]{1,2,0:T(8,128)(2,1)S(1)}, u32[]{:S(2)}, u32[]{:S(2)}) collective-permute-start(bf16[1,512,224]{1,2,0:T(8,128)(2,1)} %bitcast.107), channel_id=1, source_target_pairs={{0,3},{1,2},{2,1},{3,0},{4,7},{5,6},{6,5},{7,4},{8,11},{9,10},{10,... | collective-permute-start | bytes 688136 | tf_op jit(solution)/shard_map/ppermute | solution.py:29
  46.6 9.3 %copy-start.6 = (bf16[1,1,512,224]{2,3,0,1:T(8,128)(2,1)S(1)}, bf16[1,1,512,224]{2,3,0,1:T(8,128)(2,1)}, u32[]{:S(2)}) copy-start(bf16[1,1,512,224]{2,3,0,1:T(8,128)(2,1)} %copy.47) | copy-start | bytes 688132
  46.6 24.2 %copy-start.5 = (bf16[1,1,512,224]{2,3,0,1:T(8,128)(2,1)S(1)}, bf16[1,1,512,224]{2,3,0,1:T(8,128)(2,1)}, u32[]{:S(2)}) copy-start(bf16[1,1,512,224]{2,3,0,1:T(8,128)(2,1)} %copy.46) | copy-start | bytes 688132
  48.0 22.8 %collective-permute-start.5 = (bf16[1,512,224]{1,2,0:T(8,128)(2,1)S(1)}, bf16[1,512,224]{1,2,0:T(8,128)(2,1)S(1)}, u32[]{:S(2)}, u32[]{:S(2)}) collective-permute-start(bf16[1,512,224]{1,2,0:T(8,128)(2,1)S(1)} %bitcast.134), channel_id=1, source_target_pairs={{0,4},{1,5},{2,6},{3,7},{4,0},{5,1},{6,2},{7,3},{8,12},{9,13},{10,... | collective-permute-start | bytes 688136 | tf_op jit(solution)/shard_map/ppermute | solution.py:29
  54.3 21.5 %collective-permute-start.6 = (bf16[1,512,224]{1,2,0:T(8,128)(2,1)}, bf16[1,512,224]{1,2,0:T(8,128)(2,1)S(1)}, u32[]{:S(2)}, u32[]{:S(2)}) collective-permute-start(bf16[1,512,224]{1,2,0:T(8,128)(2,1)} %bitcast.133), channel_id=1, source_target_pairs={{0,5},{1,4},{2,7},{3,6},{4,1},{5,0},{6,3},{7,2},{8,13},{9,12},{10,... | collective-permute-start | bytes 688136 | tf_op jit(solution)/shard_map/ppermute | solution.py:29
  55.9 31.6 %collective-permute-start.7 = (bf16[1,512,224]{1,2,0:T(8,128)(2,1)S(1)}, bf16[1,512,224]{1,2,0:T(8,128)(2,1)S(1)}, u32[]{:S(2)}, u32[]{:S(2)}) collective-permute-start(bf16[1,512,224]{1,2,0:T(8,128)(2,1)S(1)} %bitcast.132), channel_id=1, source_target_pairs={{0,6},{1,7},{2,4},{3,5},{4,2},{5,3},{6,0},{7,1},{8,14},{9,15},{10,... | collective-permute-start | bytes 688136 | tf_op jit(solution)/shard_map/ppermute | solution.py:29
  70.8 21.6 %collective-permute-start.8 = (bf16[1,512,224]{1,2,0:T(8,128)(2,1)S(1)}, bf16[1,512,224]{1,2,0:T(8,128)(2,1)S(1)}, u32[]{:S(2)}, u32[]{:S(2)}) collective-permute-start(bf16[1,512,224]{1,2,0:T(8,128)(2,1)S(1)} %bitcast.131), channel_id=1, source_target_pairs={{0,7},{1,6},{2,5},{3,4},{4,3},{5,2},{6,1},{7,0},{8,15},{9,14},{10,... | collective-permute-start | bytes 688136 | tf_op jit(solution)/shard_map/ppermute | solution.py:29
  92.4 1.2 copy-start.1
  98.1 2.2 copy-start.2
  98.1 2.2 copy-start.3
  101.7 1.5 copy-start.8
  107.1 1.4 copy-start.4
  113.2 1.6 copy-start
  120.4 1.4 copy-start.4
  126.5 1.6 copy-start
  133.6 1.4 copy-start.4
  139.7 1.6 copy-start
  146.9 1.4 copy-start.4
  153.0 1.6 copy-start
  160.1 1.4 copy-start.4
  166.2 1.6 copy-start
  173.4 1.4 copy-start.4
  179.5 1.6 copy-start
  186.6 1.4 copy-start.4
  192.7 1.6 copy-start
  199.9 1.4 copy-start.4
  206.0 1.6 copy-start
  213.2 1.4 copy-start.4
  219.3 1.6 copy-start
  226.5 1.4 copy-start.4
  232.6 1.6 copy-start
  239.8 1.4 copy-start.4
  246.0 1.6 copy-start
  253.2 1.4 copy-start.4
  259.3 1.6 copy-start
  266.5 1.4 copy-start.4
  272.6 1.6 copy-start
  279.8 1.4 copy-start.4
  285.9 1.6 copy-start
  289.5 15.1 %collective-permute-start.10 = (bf16[2,512,256]{2,1,0:T(8,128)(2,1)S(1)}, bf16[2,512,256]{2,1,0:T(8,128)(2,1)S(1)}, u32[]{:S(2)}, u32[]{:S(2)}) collective-permute-start(bf16[2,512,256]{2,1,0:T(8,128)(2,1)S(1)} %pad_maximum_fusion.3), channel_id=1, source_target_pairs={{2,0},{3,1},{4,2},{5,3},{6,4},{7,5},{10,8},{11,9},{12,10},{13,11},... | collective-permute-start | bytes 1572872 | tf_op jit(solution)/shard_map/ppermute | solution.py:37
  291.7 19.0 %collective-permute-start.9 = (bf16[2,512,256]{2,1,0:T(8,128)(2,1)S(1)}, bf16[2,512,256]{2,1,0:T(8,128)(2,1)S(1)}, u32[]{:S(2)}, u32[]{:S(2)}) collective-permute-start(bf16[2,512,256]{2,1,0:T(8,128)(2,1)S(1)} %pad_maximum_fusion.2), channel_id=1, source_target_pairs={{1,0},{2,1},{3,2},{4,3},{5,4},{6,5},{7,6},{9,8},{10,9},{11,10},{12... | collective-permute-start | bytes 1572872 | tf_op jit(solution)/shard_map/ppermute | solution.py:37
